TPU v7x, 32 devices: a whole 2x2x4 slice. The times are simulated.
32 devices in a mesh: parts: 2 (over y), ctx: 4 (over z), grid: 4 (over x, core).
Axes of the slice: x: 2, y: 2, z: 4, core: 2. Of those that a mesh axis runs over, the one named last changes fastest.
Arguments:
- frames_in: bfloat16 [4096, 1536], P(('parts', 'ctx'), 'grid'), parts along dimension 0, may hold values from -230 to 230
- norm1_gain: bfloat16 [1536], P('grid'), may hold values from 0.25 to 1.75
- norm1_bias: bfloat16 [1536], P('grid'), may hold values from -3 to 3
- w_query: bfloat16 [1536, 1536], P(None, 'grid'), may hold values from -0.5 to 0.5
- w_key: bfloat16 [1536, 1536], P(None, 'grid'), may hold values from -2 to 2
- w_value: bfloat16 [1536, 1536], P(None, 'grid'), may hold values from -0.15625 to 0.15625
- w_out: bfloat16 [1536, 1536], P('grid'), may hold values from -0.15625 to 0.15625
- norm2_gain: bfloat16 [1536], P('grid'), may hold values from 0.099609375 to 1.8984375
- norm2_bias: bfloat16 [1536], P('grid'), may hold values from -3 to 3
- w_glu_value: bfloat16 [1536, 1536], P(None, 'grid'), may hold values from -0.15625 to 0.15625
- w_glu_gate: bfloat16 [1536, 1536], P(None, 'grid'), may hold values from -0.15625 to 0.15625
- depth_kernel: float32 [31, 1536], P(None, 'grid'), may hold values from -1 to 1
- bn_scale: float32 [1536], P('grid'), may hold values from 0.25 to 1.75
- bn_shift: float32 [1536], P('grid'), may hold values from -3 to 3
- w_proj: bfloat16 [1536, 1536], P('grid'), may hold values from -0.3125 to 0.3125
Outputs:
- layer_out: bfloat16 [4096, 1536], P(('parts', 'ctx'), 'grid'), parts along dimension 0
There are 2 independent parts, one for each index of `parts`. A program takes and returns all parts, laid end to end along the dimension named above; an argument that names none is the same for every part. Nothing has to cross between parts.
All inputs are finite; a program needn't handle non-finite values.
Results may differ from a plain program's by a relative error of at most 0.009.
Values may be sent and summed in bfloat16 or wider, within the bound.
A program may use at most 256 MiB of HBM per device.

v0:
```python
import math
import jax
import jax.numpy as jnp
from jax import lax
from jax.sharding import PartitionSpec as P

HEAD_DIM = 64
KERNEL = 31
HALF = 15
EPSILON = 1e-05
NEG_LARGE = -1e30


def with_halo(cells, sides, width):
    for axis, dim in sides:
        count = lax.axis_size(axis)
        ends = count - 1
        head = lax.slice_in_dim(cells, 0, width, axis=dim)
        tail = lax.slice_in_dim(cells, cells.shape[dim] - width, cells.shape[dim], axis=dim)
        cells = jnp.concatenate(
            [
                lax.ppermute(tail, axis, [(i, (i + 1) % count) for i in range(ends)]),
                cells,
                lax.ppermute(head, axis, [((i + 1) % count, i) for i in range(ends)]),
            ],
            axis=dim,
        )
    return cells


def attend_block(state, query_heads, key_block, value_block):
    row_max, row_sum, weighted = state
    heads_dev = query_heads.shape[1]
    key_heads = key_block.reshape(key_block.shape[0], heads_dev, HEAD_DIM)
    value_heads = value_block.reshape(value_block.shape[0], heads_dev, HEAD_DIM)
    scores = jnp.einsum(
        "qhd,khd->hqk", query_heads, key_heads, preferred_element_type=jnp.float32
    ) * (1.0 / math.sqrt(HEAD_DIM))
    new_max = jnp.maximum(row_max, jnp.max(scores, axis=2))
    factor = jnp.exp(row_max - new_max)
    soft_weights = jnp.exp(scores - new_max[:, :, None])
    new_sum = row_sum * factor + jnp.sum(soft_weights, axis=2)
    mixed = jnp.einsum(
        "hqk,khd->qhd",
        soft_weights.astype(jnp.bfloat16),
        value_heads,
        preferred_element_type=jnp.float32,
    )
    mixed = mixed.reshape(mixed.shape[0], heads_dev * HEAD_DIM)
    weighted = weighted * jnp.repeat(jnp.transpose(factor), HEAD_DIM, axis=1) + mixed
    return (new_max, new_sum, weighted)


def attend_keys(state, query_heads, key_rows, value_rows):
    key_count = key_rows.shape[0]
    block_rows = math.gcd(key_count, 512)

    def loop_step(block_index, carried):
        key_block = lax.dynamic_slice_in_dim(key_rows, block_index * block_rows, block_rows, 0)
        value_block = lax.dynamic_slice_in_dim(value_rows, block_index * block_rows, block_rows, 0)
        return attend_block(carried, query_heads, key_block, value_block)

    return lax.fori_loop(0, key_count // block_rows, loop_step, state)


def project_normed(local_shard, gain_shard, shift_shard, weights):
    values = local_shard.astype(jnp.float32)
    full_width = values.shape[1] * lax.axis_size("grid")
    totals = lax.psum((jnp.sum(values, axis=1), jnp.sum(values * values, axis=1)), "grid")
    row_mean = totals[0] / full_width
    variance = totals[1] / full_width - row_mean * row_mean
    scaled = (values - row_mean[:, None]) * lax.rsqrt(variance + EPSILON)[:, None]
    normed = (scaled * gain_shard.astype(jnp.float32) + shift_shard.astype(jnp.float32)).astype(
        jnp.bfloat16
    )
    block_piece = lax.all_gather(normed, "grid", axis=1, tiled=True)
    return tuple(
        (jnp.dot(block_piece, weight, preferred_element_type=jnp.float32) for weight in weights)
    )


def branch_sum(activation, weight_rows):
    share = lax.psum_scatter(
        lax.dot_general(
            weight_rows, activation, (((0,), (1,)), ((), ())), preferred_element_type=jnp.float32
        ).astype(jnp.bfloat16),
        "grid",
        scatter_dimension=0,
        tiled=True,
    ).astype(jnp.float32)
    return jnp.transpose(share)


def on_device(
    frames_in,
    norm1_gain,
    norm1_bias,
    w_query,
    w_key,
    w_value,
    w_out,
    norm2_gain,
    norm2_bias,
    w_glu_value,
    w_glu_gate,
    depth_kernel,
    bn_scale,
    bn_shift,
    w_proj,
):
    local_frames = frames_in.shape[0]
    heads_dev = w_query.shape[1] // HEAD_DIM
    head_width = heads_dev * HEAD_DIM
    query_full, key_full, value_full = project_normed(
        frames_in, norm1_gain, norm1_bias, (w_query, w_key, w_value)
    )
    query_rows = query_full.astype(jnp.bfloat16)
    key_rows = key_full.astype(jnp.bfloat16)
    value_rows = value_full.astype(jnp.bfloat16)
    query_heads = query_rows.reshape(local_frames, heads_dev, HEAD_DIM)
    start_state = (
        jnp.full((heads_dev, local_frames), NEG_LARGE, jnp.float32),
        jnp.zeros((heads_dev, local_frames), jnp.float32),
        jnp.zeros((local_frames, head_width), jnp.float32),
    )
    final_max, final_sum, weighted = attend_keys(
        start_state,
        query_heads,
        lax.all_gather(key_rows, "ctx", axis=0, tiled=True),
        lax.all_gather(value_rows, "ctx", axis=0, tiled=True),
    )
    attended = (weighted / jnp.repeat(jnp.transpose(final_sum), HEAD_DIM, axis=1)).astype(
        jnp.bfloat16
    )
    middle = (frames_in.astype(jnp.float32) + branch_sum(attended, w_out)).astype(jnp.bfloat16)
    value_part, gate_part = project_normed(
        middle, norm2_gain, norm2_bias, (w_glu_value, w_glu_gate)
    )
    gated = (value_part * jax.nn.sigmoid(gate_part)).astype(jnp.bfloat16)
    padded = with_halo(gated, (("ctx", 0),), HALF)
    convolved = jnp.zeros((local_frames, gated.shape[1]), jnp.float32)
    for tap_index in range(KERNEL):
        convolved = convolved + depth_kernel[tap_index] * padded[
            tap_index : tap_index + local_frames
        ].astype(jnp.float32)
    activated = jax.nn.silu(convolved * bn_scale + bn_shift).astype(jnp.bfloat16)
    return (middle.astype(jnp.float32) + branch_sum(activated, w_proj)).astype(jnp.bfloat16)


def solution(mesh):
    return jax.shard_map(
        on_device,
        mesh=mesh,
        in_specs=(
            P(("parts", "ctx"), "grid"),
            P("grid"),
            P("grid"),
            P(None, "grid"),
            P(None, "grid"),
            P(None, "grid"),
            P("grid", None),
            P("grid"),
            P("grid"),
            P(None, "grid"),
            P(None, "grid"),
            P(None, "grid"),
            P("grid"),
            P("grid"),
            P("grid", None),
        ),
        out_specs=P(("parts", "ctx"), "grid"),
        check_vma=False,
    )
```

profile of v0, /device:TPU:0, one launch (start us, length us, event | category | flops | bytes accessed | tf_op | source)
XLA Modules:
  0.0 290.1 jit_solution(2642509837750959536)
XLA Ops:
  9.2 8.3 %all-reduce.1 = (f32[512]{0:T(512)S(1)}, f32[512]{0:T(512)S(1)}) all-reduce(f32[512]{0:T(512)S(1)} %get-tuple-element.173, f32[512]{0:T(512)S(1)} %get-tuple-element.172), channel_id=1, replica_groups=mesh['parts'=2,'ctx'=4,'grid'=4] {'grid'}, use_global_device_ids=true, to_apply=%region_3.0 | all-reduce | flops 1024 | bytes 8192 | tf_op jit(solution)/shard_map/psum | solution.py:69
  19.6 20.1 %all-gather.5.cloned.1.call-done = bf16[512,1536]{1,0:T(8,128)(2,1)} async-done(((bf16[512,384]{1,0:T(8,128)(2,1)}), bf16[512,1536]{1,0:T(8,128)(2,1)}) %all-gather.5.cloned.1.call-update) | async-done | bytes 1572880 | tf_op jit(solution)/shard_map/all_gather | solution.py:76
  39.7 3.6 %convolution_convert_fusion.4 = bf16[512,384]{1,0:T(8,128)(2,1)} fusion(bf16[512,1536]{1,0:T(8,128)(2,1)} %all-gather.5.cloned.1.call-done, bf16[1536,384]{1,0:T(8,128)(2,1)} %param.21), kind=kOutput, calls=%fused_computation.66 | convolution fusion | flops 604176384 | bytes 3145728 | tf_op jit(solution)/shard_map/dot_general | solution.py:78
  49.0 31.5 %all-gather.7.cloned.1.call-done = bf16[2048,384]{1,0:T(8,128)(2,1)} async-done(((bf16[512,384]{1,0:T(8,128)(2,1)}), bf16[2048,384]{1,0:T(8,128)(2,1)}) %all-gather.7.cloned.1.call-update) | async-done | bytes 1572880 | tf_op jit(solution)/shard_map/all_gather | solution.py:129
  80.6 37.6 %all-gather.9.cloned.1.call-done = bf16[2048,384]{1,0:T(8,128)(2,1)} async-done(((bf16[512,384]{1,0:T(8,128)(2,1)}), bf16[2048,384]{1,0:T(8,128)(2,1)}) %all-gather.9.cloned.1.call-update) | async-done | bytes 1572880 | tf_op jit(solution)/shard_map/all_gather | solution.py:130
  118.1 53.8 %while.18 = (s32[]{:T(128)}, f32[6,512]{1,0:T(8,128)S(1)}, f32[6,512]{1,0:T(8,128)}, f32[512,384]{0,1:T(8,128)S(1)}, bf16[2048,384]{1,0:T(8,128)(2,1)}, /*index=...) while((s32[]{:T(128)}, f32[6,512]{1,0:T(8,128)S(1)}, ...), condition=%wide.region_7.0_spmd.clone, body=%wide.region_4.0_spmd.clone.sunk | while | flops 415844352 | bytes 26640616 | solution.py:63
  119.5 3.7 %bitcast_reduce_fusion.2 = (f32[6,512]{1,0:T(8,128)S(1)}, f32[6,512,512]{2,1,0:T(8,128)}) fusion(bf16[512,6,64]{0,2,1:T(8,128)(2,1)S(1)} %bitcast.78, bf16[512,6,64]{0,2,1:T(8,128)(2,1)S(1)} %get-tuple-element.318), kind=kOutput, calls=%fused_computation.1.clone.1 | convolution fusion | flops 204469248 | bytes 7090176 | tf_op jit(solution)/shard_map/while/body/eval_jaxpr/qhd,khd->hqk/dot_general | solution.py:36
  123.2 3.8 %fusion.90 = f32[6,512]{1,0:T(8,128)S(1)} fusion(f32[6,512,512]{2,1,0:T(8,128)} %get-tuple-element.288, f32[6,512]{1,0:T(8,128)S(1)} %get-tuple-element.314), kind=kLoop, calls=%fused_computation.4.clone.1 | loop fusion | flops 4715520 | bytes 6316032 | tf_op jit(solution)/shard_map/while/body/eval_jaxpr/reduce_sum | solution.py:42
  127.3 4.0 %fusion.92 = f32[6,64,512]{2,1,0:T(8,128)S(1)} fusion(bf16[512,6,64]{0,2,1:T(8,128)(2,1)S(1)} %bitcast.77, f32[6,512,512]{2,1,0:T(8,128)} %get-tuple-element.288, f32[6,512]{1,0:T(8,128)S(1)} %get-tuple-element.314), kind=kOutput, calls=%fused_computation.5.clone.1 | convolution fusion | flops 206045184 | bytes 7483392 | tf_op jit(solution)/shard_map/while/body/eval_jaxpr/hqk,khd->qhd/dot_general | solution.py:43
  133.0 3.7 %bitcast_reduce_fusion.2 = (f32[6,512]{1,0:T(8,128)S(1)}, f32[6,512,512]{2,1,0:T(8,128)}) fusion(bf16[512,6,64]{0,2,1:T(8,128)(2,1)S(1)} %bitcast.78, bf16[512,6,64]{0,2,1:T(8,128)(2,1)S(1)} %get-tuple-element.318), kind=kOutput, calls=%fused_computation.1.clone.1 | convolution fusion | flops 204469248 | bytes 7090176 | tf_op jit(solution)/shard_map/while/body/eval_jaxpr/qhd,khd->hqk/dot_general | solution.py:36
  136.7 3.8 %fusion.90 = f32[6,512]{1,0:T(8,128)S(1)} fusion(f32[6,512,512]{2,1,0:T(8,128)} %get-tuple-element.288, f32[6,512]{1,0:T(8,128)S(1)} %get-tuple-element.314), kind=kLoop, calls=%fused_computation.4.clone.1 | loop fusion | flops 4715520 | bytes 6316032 | tf_op jit(solution)/shard_map/while/body/eval_jaxpr/reduce_sum | solution.py:42
  140.8 4.0 %fusion.92 = f32[6,64,512]{2,1,0:T(8,128)S(1)} fusion(bf16[512,6,64]{0,2,1:T(8,128)(2,1)S(1)} %bitcast.77, f32[6,512,512]{2,1,0:T(8,128)} %get-tuple-element.288, f32[6,512]{1,0:T(8,128)S(1)} %get-tuple-element.314), kind=kOutput, calls=%fused_computation.5.clone.1 | convolution fusion | flops 206045184 | bytes 7483392 | tf_op jit(solution)/shard_map/while/body/eval_jaxpr/hqk,khd->qhd/dot_general | solution.py:43
  146.4 3.7 %bitcast_reduce_fusion.2 = (f32[6,512]{1,0:T(8,128)S(1)}, f32[6,512,512]{2,1,0:T(8,128)}) fusion(bf16[512,6,64]{0,2,1:T(8,128)(2,1)S(1)} %bitcast.78, bf16[512,6,64]{0,2,1:T(8,128)(2,1)S(1)} %get-tuple-element.318), kind=kOutput, calls=%fused_computation.1.clone.1 | convolution fusion | flops 204469248 | bytes 7090176 | tf_op jit(solution)/shard_map/while/body/eval_jaxpr/qhd,khd->hqk/dot_general | solution.py:36
  150.1 3.8 %fusion.90 = f32[6,512]{1,0:T(8,128)S(1)} fusion(f32[6,512,512]{2,1,0:T(8,128)} %get-tuple-element.288, f32[6,512]{1,0:T(8,128)S(1)} %get-tuple-element.314), kind=kLoop, calls=%fused_computation.4.clone.1 | loop fusion | flops 4715520 | bytes 6316032 | tf_op jit(solution)/shard_map/while/body/eval_jaxpr/reduce_sum | solution.py:42
  154.2 4.0 %fusion.92 = f32[6,64,512]{2,1,0:T(8,128)S(1)} fusion(bf16[512,6,64]{0,2,1:T(8,128)(2,1)S(1)} %bitcast.77, f32[6,512,512]{2,1,0:T(8,128)} %get-tuple-element.288, f32[6,512]{1,0:T(8,128)S(1)} %get-tuple-element.314), kind=kOutput, calls=%fused_computation.5.clone.1 | convolution fusion | flops 206045184 | bytes 7483392 | tf_op jit(solution)/shard_map/while/body/eval_jaxpr/hqk,khd->qhd/dot_general | solution.py:43
  159.9 3.7 %bitcast_reduce_fusion.2 = (f32[6,512]{1,0:T(8,128)S(1)}, f32[6,512,512]{2,1,0:T(8,128)}) fusion(bf16[512,6,64]{0,2,1:T(8,128)(2,1)S(1)} %bitcast.78, bf16[512,6,64]{0,2,1:T(8,128)(2,1)S(1)} %get-tuple-element.318), kind=kOutput, calls=%fused_computation.1.clone.1 | convolution fusion | flops 204469248 | bytes 7090176 | tf_op jit(solution)/shard_map/while/body/eval_jaxpr/qhd,khd->hqk/dot_general | solution.py:36
  163.6 3.8 %fusion.90 = f32[6,512]{1,0:T(8,128)S(1)} fusion(f32[6,512,512]{2,1,0:T(8,128)} %get-tuple-element.288, f32[6,512]{1,0:T(8,128)S(1)} %get-tuple-element.314), kind=kLoop, calls=%fused_computation.4.clone.1 | loop fusion | flops 4715520 | bytes 6316032 | tf_op jit(solution)/shard_map/while/body/eval_jaxpr/reduce_sum | solution.py:42
  167.7 4.0 %fusion.92 = f32[6,64,512]{2,1,0:T(8,128)S(1)} fusion(bf16[512,6,64]{0,2,1:T(8,128)(2,1)S(1)} %bitcast.77, f32[6,512,512]{2,1,0:T(8,128)} %get-tuple-element.288, f32[6,512]{1,0:T(8,128)S(1)} %get-tuple-element.314), kind=kOutput, calls=%fused_computation.5.clone.1 | convolution fusion | flops 206045184 | bytes 7483392 | tf_op jit(solution)/shard_map/while/body/eval_jaxpr/hqk,khd->qhd/dot_general | solution.py:43
  176.1 26.5 %reduce-scatter.7.cloned.1.call-done = bf16[384,512]{1,0:T(8,128)(2,1)} async-done(((bf16[1536,512]{1,0:T(8,128)(2,1)}), bf16[384,512]{1,0:T(8,128)(2,1)}) %reduce-scatter.7.cloned.1.call-update) | async-done | bytes 393232
  204.1 5.8 %all-reduce = (f32[512]{0:T(512)S(1)}, f32[512]{0:T(512)S(1)}) all-reduce(f32[512]{0:T(512)S(1)} %get-tuple-element.171, f32[512]{0:T(512)S(1)} %get-tuple-element.170), channel_id=1, replica_groups=mesh['parts'=2,'ctx'=4,'grid'=4] {'grid'}, use_global_device_ids=true, to_apply=%region_12.0 | all-reduce | flops 1024 | bytes 8192 | tf_op jit(solution)/shard_map/psum | solution.py:69
  211.0 20.7 %all-gather.11.cloned.1.call-done = bf16[512,1536]{1,0:T(8,128)(2,1)} async-done(((bf16[512,384]{1,0:T(8,128)(2,1)}), bf16[512,1536]{1,0:T(8,128)(2,1)}) %all-gather.11.cloned.1.call-update) | async-done | bytes 1572880 | tf_op jit(solution)/shard_map/all_gather | solution.py:76
  237.0 4.7 %collective-permute-start = (bf16[15,384]{1,0:T(8,128)(2,1)S(1)}, bf16[15,384]{1,0:T(8,128)(2,1)S(1)}, u32[]{:S(2)}, u32[]{:S(2)}) collective-permute-start(bf16[15,384]{1,0:T(8,128)(2,1)S(1)} %get-tuple-element.230), channel_id=1, source_target_pairs={{0,4},{4,8},{8,12},{1,5},{5,9},{9,13},{2,6},{6,10},{10,14},{3,7},{... | collective-permute-start | bytes 34568 | tf_op jit(solution)/shard_map/ppermute | solution.py:22
  243.0 7.4 %fusion.11 = bf16[1536,512]{0,1:T(8,128)(2,1)S(1)} fusion(bf16[384,1536]{1,0:T(8,128)(2,1)S(1)} %copy-done.10, bf16[512,384]{1,0:T(8,128)(2,1)S(1)} %fusion.15, bf16[15,384]{1,0:T(8,128)(2,1)S(1)} %collective-permute-done.1, bf16[15,384]{1,0:T(8,128)(2,1)S(1)} %collective-permute-done, f32[384]{0:T(512)S(1)} %copy-done.11, f32[384]{0:T(512)S(1)} %copy-done.12, ...), kind=kOutput, calls=%fused_computation.21 | convolution fusion | flops 641925120 | bytes 3219456 | tf_op jit(solution)/shard_map/dot_general | solution.py:84
  252.0 29.2 %reduce-scatter.9.cloned.1.call-done = bf16[384,512]{1,0:T(8,128)(2,1)} async-done(((bf16[1536,512]{1,0:T(8,128)(2,1)}), bf16[384,512]{1,0:T(8,128)(2,1)}) %reduce-scatter.9.cloned.1.call-update) | async-done | bytes 393232
  (108 shorter events, 34.7 us)
Async XLA Ops:
  6.5 166.2 %copy-start = (bf16[384,1536]{1,0:T(8,128)(2,1)S(1)}, bf16[384,1536]{1,0:T(8,128)(2,1)}, u32[]{:S(2)}) copy-start(bf16[384,1536]{1,0:T(8,128)(2,1)} %param.23) | copy-start | bytes 3538948
  6.5 33.1 %all-gather.5.cloned.1.call-start = ((), (), s32[]{:S(2)}) async-start(), calls=%async_computation.2 | async-start | bytes 1966080 | tf_op jit(solution)/shard_map/all_gather | solution.py:76
  19.6 61.0 %all-gather.7.cloned.1.call-start = ((), (), s32[]{:S(2)}) async-start(), calls=%async_computation.3 | async-start | bytes 1966080 | tf_op jit(solution)/shard_map/all_gather | solution.py:129
  39.7 3.7 %copy-start.7 = (bf16[512,1536]{1,0:T(8,128)(2,1)S(1)}, bf16[512,1536]{1,0:T(8,128)(2,1)}, u32[]{:S(2)}) copy-start(bf16[512,1536]{1,0:T(8,128)(2,1)} %all-gather.5.cloned.1.call-done) | copy-start | bytes 4718596
  43.3 74.8 %all-gather.9.cloned.1.call-start = ((), (), s32[]{:S(2)}) async-start(), calls=%async_computation.4 | async-start | bytes 1966080 | tf_op jit(solution)/shard_map/all_gather | solution.py:130
  46.4 156.2 %reduce-scatter.7.cloned.1.call-start = ((), (), s32[]{:S(2)}) async-start(), calls=%async_computation.6 | async-start | bytes 1966080
  123.2 3.8 %copy-start.2 = (f32[6,512]{1,0:T(8,128)S(1)}, f32[6,512]{1,0:T(8,128)}, u32[]{:S(2)}) copy-start(f32[6,512]{1,0:T(8,128)} %get-tuple-element.304) | copy-start | bytes 36868 | tf_op jit(solution)/shard_map/while
  127.1 4.5 %copy-start.3 = (f32[6,512]{1,0:T(8,128)}, f32[6,512]{1,0:T(8,128)S(1)}, u32[]{:S(2)}) copy-start(f32[6,512]{1,0:T(8,128)S(1)} %fusion.91) | copy-start | bytes 36868 | tf_op jit(solution)/shard_map/while
  136.7 3.8 %copy-start.2 = (f32[6,512]{1,0:T(8,128)S(1)}, f32[6,512]{1,0:T(8,128)}, u32[]{:S(2)}) copy-start(f32[6,512]{1,0:T(8,128)} %get-tuple-element.304) | copy-start | bytes 36868 | tf_op jit(solution)/shard_map/while
  140.5 4.5 %copy-start.3 = (f32[6,512]{1,0:T(8,128)}, f32[6,512]{1,0:T(8,128)S(1)}, u32[]{:S(2)}) copy-start(f32[6,512]{1,0:T(8,128)S(1)} %fusion.91) | copy-start | bytes 36868 | tf_op jit(solution)/shard_map/while
  150.1 3.8 %copy-start.2 = (f32[6,512]{1,0:T(8,128)S(1)}, f32[6,512]{1,0:T(8,128)}, u32[]{:S(2)}) copy-start(f32[6,512]{1,0:T(8,128)} %get-tuple-element.304) | copy-start | bytes 36868 | tf_op jit(solution)/shard_map/while
  154.0 4.5 %copy-start.3 = (f32[6,512]{1,0:T(8,128)}, f32[6,512]{1,0:T(8,128)S(1)}, u32[]{:S(2)}) copy-start(f32[6,512]{1,0:T(8,128)S(1)} %fusion.91) | copy-start | bytes 36868 | tf_op jit(solution)/shard_map/while
  163.6 3.8 %copy-start.2 = (f32[6,512]{1,0:T(8,128)S(1)}, f32[6,512]{1,0:T(8,128)}, u32[]{:S(2)}) copy-start(f32[6,512]{1,0:T(8,128)} %get-tuple-element.304) | copy-start | bytes 36868 | tf_op jit(solution)/shard_map/while
  167.5 4.5 %copy-start.3 = (f32[6,512]{1,0:T(8,128)}, f32[6,512]{1,0:T(8,128)S(1)}, u32[]{:S(2)}) copy-start(f32[6,512]{1,0:T(8,128)S(1)} %fusion.91) | copy-start | bytes 36868 | tf_op jit(solution)/shard_map/while
  175.4 28.4 %copy-start.1 = (bf16[512,384]{1,0:T(8,128)(2,1)S(1)}, bf16[512,384]{1,0:T(8,128)(2,1)}, u32[]{:S(2)}) copy-start(bf16[512,384]{1,0:T(8,128)(2,1)} %param.17) | copy-start | bytes 1179652
  175.4 56.3 %all-gather.11.cloned.1.call-start = ((), (), s32[]{:S(2)}) async-start(), calls=%async_computation.5 | async-start | bytes 1966080 | tf_op jit(solution)/shard_map/all_gather | solution.py:76
  176.1 34.8 %copy-start.4 = (f32[31,384]{1,0:T(8,128)S(1)}, f32[31,384]{1,0:T(8,128)}, u32[]{:S(2)}) copy-start(f32[31,384]{1,0:T(8,128)} %param.28) | copy-start | bytes 142852
  210.8 70.4 %reduce-scatter.9.cloned.1.call-start = ((), (), s32[]{:S(2)}) async-start(), calls=%async_computation.7 | async-start | bytes 1966080
  231.7 3.0 %copy-start.9 = (bf16[1536,384]{1,0:T(8,128)(2,1)S(1)}, bf16[1536,384]{1,0:T(8,128)(2,1)}, u32[]{:S(2)}) copy-start(bf16[1536,384]{1,0:T(8,128)(2,1)} %param.26) | copy-start | bytes 3538948
  234.7 8.3 %copy-start.10 = (bf16[384,1536]{1,0:T(8,128)(2,1)S(1)}, bf16[384,1536]{1,0:T(8,128)(2,1)}, u32[]{:S(2)}) copy-start(bf16[384,1536]{1,0:T(8,128)(2,1)} %param.31) | copy-start | bytes 3538948
  234.7 8.3 %copy-start.11 = (f32[384]{0:T(512)S(1)}, f32[384]{0:T(512)}, u32[]{:S(2)}) copy-start(f32[384]{0:T(512)} %param.30) | copy-start | bytes 4612
  234.7 8.3 %copy-start.12 = (f32[384]{0:T(512)S(1)}, f32[384]{0:T(512)}, u32[]{:S(2)}) copy-start(f32[384]{0:T(512)} %param.29) | copy-start | bytes 4612
  235.7 6.1 %collective-permute-start.1 = (bf16[15,384]{1,0:T(8,128)(2,1)S(1)}, bf16[15,384]{1,0:T(8,128)(2,1)S(1)}, u32[]{:S(2)}, u32[]{:S(2)}) collective-permute-start(bf16[15,384]{1,0:T(8,128)(2,1)S(1)} %get-tuple-element.231), channel_id=1, source_target_pairs={{4,0},{8,4},{12,8},{5,1},{9,5},{13,9},{6,2},{10,6},{14,10},{7,3},{... | collective-permute-start | bytes 34568 | tf_op jit(solution)/shard_map/ppermute | solution.py:24
  237.0 5.9 %collective-permute-start = (bf16[15,384]{1,0:T(8,128)(2,1)S(1)}, bf16[15,384]{1,0:T(8,128)(2,1)S(1)}, u32[]{:S(2)}, u32[]{:S(2)}) collective-permute-start(bf16[15,384]{1,0:T(8,128)(2,1)S(1)} %get-tuple-element.230), channel_id=1, source_target_pairs={{0,4},{4,8},{8,12},{1,5},{5,9},{9,13},{2,6},{6,10},{10,14},{3,7},{... | collective-permute-start | bytes 34568 | tf_op jit(solution)/shard_map/ppermute | solution.py:22
  (3 other events, 4.3 us)
Sparse Core Ops, SparseCore 0:
  19.7 19.9 all-gather.4
  43.4 37.0 all-gather.6
  82.1 35.9 all-gather.8
  175.5 27.0 reduce-scatter.6
  211.0 20.7 all-gather.10
  252.1 29.0 reduce-scatter.8
where the time goes:
time: 291 us; the launch traced here: 290 us
  waiting for transfers between devices  167 us (57%)
  matrix products  52.1 us (18%)
  other arithmetic  24 us (8%)
  blocking collectives  14.1 us (5%)
  between operations  13.7 us (5%)
  local copies, waits for them, and re-layouts  12.8 us (4%)
  starting transfers between devices  6.23 us (2%)
    unnamed x8, waiting for transfers between devices  55.8 us
    all_gather x2, waiting for transfers between devices, project_normed(): block_piece = lax.all_gather(normed, 'grid', axis=1, tiled=True)  40.8 us
    all_gather x1, waiting for transfers between devices, on_device(): lax.all_gather(value_rows, 'ctx', axis=0, tiled=True)  37.6 us
    all_gather x1, waiting for transfers between devices, on_device(): lax.all_gather(key_rows, 'ctx', axis=0, tiled=True)  31.5 us
    dot_general x4, matrix products, attend_block(): jnp.einsum('hqk,khd->qhd', soft_weights.astype(jnp.bfloat16), value_heads...  15.9 us
    reduce_sum x4, other arithmetic, attend_block(): new_sum = row_sum * factor + jnp.sum(soft_weights, axis=2)  15.3 us
    dot_general x4, matrix products, attend_block(): jnp.einsum('qhd,khd->hqk', query_heads, key_heads, preferred_element_type...  14.8 us
    psum x2, blocking collectives, project_normed(): lax.psum((jnp.sum(values, axis=1), jnp.sum(values * values, axis=1)), 'gr...  14.1 us
  transfers between devices with their start and end apart: 8, of which 7 were waited for; matrix products, arithmetic and copies ran while one was open for 2% of the time, Pallas kernels for 0%

commit v1 on v0

--- a/solution.py
+++ b/solution.py
@@ -9,6 +9,24 @@
 HALF = 15
 EPSILON = 1e-05
 NEG_LARGE = -1e30
+
+
+def gather_around(array, axis, dim):
+    ways, here, hop = (lax.axis_size(axis), lax.axis_index(axis), array.shape[dim])
+    dims = [n * ways if d == dim else n for d, n in enumerate(array.shape)]
+    full = lax.dynamic_update_slice_in_dim(
+        jnp.zeros(dims, array.dtype), array, here * hop, axis=dim
+    )
+    going_up = going_down = array
+    for far in range(1, ways // 2 + 1):
+        going_up = lax.ppermute(going_up, axis, [(d, (d + 1) % ways) for d in range(ways)])
+        full = lax.dynamic_update_slice_in_dim(full, going_up, (here - far) % ways * hop, axis=dim)
+        if 2 * far < ways:
+            going_down = lax.ppermute(going_down, axis, [(d, (d - 1) % ways) for d in range(ways)])
+            full = lax.dynamic_update_slice_in_dim(
+                full, going_down, (here + far) % ways * hop, axis=dim
+            )
+    return full
 
 
 def with_halo(cells, sides, width):
@@ -126,7 +144,7 @@
     final_max, final_sum, weighted = attend_keys(
         start_state,
         query_heads,
-        lax.all_gather(key_rows, "ctx", axis=0, tiled=True),
+        gather_around(key_rows, "ctx", 0),
         lax.all_gather(value_rows, "ctx", axis=0, tiled=True),
     )
     attended = (weighted / jnp.repeat(jnp.transpose(final_sum), HEAD_DIM, axis=1)).astype(

time: 291 us -> 277 us (0.952)
  waiting for transfers between devices: 167 us -> 130 us
  starting transfers between devices: 6.23 us -> 19.5 us
  local copies, waits for them, and re-layouts: 12.8 us -> 24 us
    all_gather x1, waiting for transfers between devices: 37.6 us -> 2.85 us  [on_device(): lax.all_gather(value_rows, 'ctx', axis=0, tiled=True)]
    all_gather x1 -> x0, waiting for transfers between devices: 31.5 us -> none  [on_device(): lax.all_gather(key_rows, 'ctx', axis=0, tiled=True)]
    ppermute x0 -> x3, waiting for transfers between devices: none -> 28.3 us  [the longest x2 20.2 us: gather_around(): lax.ppermute(going_up, axis, [(d, (d + 1) % ways) for d in range(ways)])]
    ppermute x0 -> x3, starting transfers between devices: none -> 13.4 us  [the longest x2 11 us: gather_around(): lax.ppermute(going_up, axis, [(d, (d + 1) % ways) for d in range(ways)])]
    ppermute x0 -> x3, local copies, waits for them, and re-layouts: none -> 3.49 us  [the longest x2 2.33 us: gather_around(): lax.ppermute(going_up, axis, [(d, (d + 1) % ways) for d in range(ways)])]
    dynamic_update_slice x0 -> x4, local copies, waits for them, and re-layouts: none -> 3.39 us  [the longest x2 1.69 us: gather_around(): lax.dynamic_update_slice_in_dim(full, going_up, (here - far) % ways * hop...]
    dynamic_slice x4, local copies, waits for them, and re-layouts: 0.76 us -> 4.1 us  [loop_step(): lax.dynamic_slice_in_dim(key_rows, block_index * block_rows, block_rows, 0)]
    unnamed x8 -> x7, waiting for transfers between devices: 55.8 us -> 56.9 us
  transfers between devices with their start and end apart: 8 -> 10, of which waited for: 7 -> 9; matrix products, arithmetic and copies ran while one was open for 2% -> 5% of each run, Pallas kernels for 0% -> 0%
where the time goes in v1:
time: 277 us; the launch traced here: 276 us
  waiting for transfers between devices  130 us (47%)
  matrix products  51.3 us (19%)
  local copies, waits for them, and re-layouts  24 us (9%)
  other arithmetic  23.3 us (8%)
  starting transfers between devices  19.5 us (7%)
  blocking collectives  14.1 us (5%)
  between operations  13.4 us (5%)
    unnamed x7, waiting for transfers between devices  56.9 us
    all_gather x2, waiting for transfers between devices, project_normed(): block_piece = lax.all_gather(normed, 'grid', axis=1, tiled=True)  40.8 us
    ppermute x2, waiting for transfers between devices, gather_around(): lax.ppermute(going_up, axis, [(d, (d + 1) % ways) for d in range(ways)])  20.2 us
    dot_general x4, matrix products, attend_block(): jnp.einsum('hqk,khd->qhd', soft_weights.astype(jnp.bfloat16), value_heads...  15.9 us
    reduce_sum x4, other arithmetic, attend_block(): new_sum = row_sum * factor + jnp.sum(soft_weights, axis=2)  15.3 us
    dot_general x4, matrix products, attend_block(): jnp.einsum('qhd,khd->hqk', query_heads, key_heads, preferred_element_type...  14.8 us
    psum x2, blocking collectives, project_normed(): lax.psum((jnp.sum(values, axis=1), jnp.sum(values * values, axis=1)), 'gr...  14.1 us
    dot_general x5, matrix products, project_normed(): jnp.dot(block_piece, weight, preferred_element_type=jnp.float32)  12.3 us
  transfers between devices with their start and end apart: 10, of which 9 were waited for; matrix products, arithmetic and copies ran while one was open for 5% of the time, Pallas kernels for 0%

profile of v1, /device:TPU:0, one launch (start us, length us, event | category | flops | bytes accessed | tf_op | source)
XLA Modules:
  0.0 275.9 jit_solution(8052030082672491416)
XLA Ops:
  9.2 8.3 %all-reduce.1 = (f32[512]{0:T(512)S(1)}, f32[512]{0:T(512)S(1)}) all-reduce(f32[512]{0:T(512)S(1)} %get-tuple-element.173, f32[512]{0:T(512)S(1)} %get-tuple-element.172), channel_id=1, replica_groups=mesh['parts'=2,'ctx'=4,'grid'=4] {'grid'}, use_global_device_ids=true, to_apply=%region_3.0 | all-reduce | flops 1024 | bytes 8192 | tf_op jit(solution)/shard_map/psum | solution.py:87
  19.6 20.1 %all-gather.4.cloned.1.call-done = bf16[512,1536]{1,0:T(8,128)(2,1)} async-done(((bf16[512,384]{1,0:T(8,128)(2,1)}), bf16[512,1536]{1,0:T(8,128)(2,1)}) %all-gather.4.cloned.1.call-update) | async-done | bytes 1572880 | tf_op jit(solution)/shard_map/all_gather | solution.py:94
  49.5 13.8 %collective-permute-done = bf16[512,384]{1,0:T(8,128)(2,1)} collective-permute-done((bf16[512,384]{1,0:T(8,128)(2,1)S(1)}, bf16[512,384]{1,0:T(8,128)(2,1)}, u32[]{:S(2)}, u32[]{:S(2)}) %collective-permute-start) | collective-permute-done | bytes 393248 | tf_op jit(solution)/shard_map/ppermute | solution.py:22
  63.3 9.5 %collective-permute-start.2 = (bf16[512,384]{1,0:T(8,128)(2,1)}, bf16[512,384]{1,0:T(8,128)(2,1)}, u32[]{:S(2)}, u32[]{:S(2)}) collective-permute-start(bf16[512,384]{1,0:T(8,128)(2,1)} %collective-permute-done), channel_id=1, source_target_pairs={{0,4},{4,8},{8,12},{12,0},{1,5},{5,9},{9,13},{13,1},{2,6},{6,10},{... | collective-permute-start | bytes 1179656 | tf_op jit(solution)/shard_map/ppermute | solution.py:22
  78.9 8.1 %collective-permute-done.1 = bf16[512,384]{1,0:T(8,128)(2,1)} collective-permute-done((bf16[512,384]{1,0:T(8,128)(2,1)S(1)}, bf16[512,384]{1,0:T(8,128)(2,1)}, u32[]{:S(2)}, u32[]{:S(2)}) %collective-permute-start.1) | collective-permute-done | bytes 393248 | tf_op jit(solution)/shard_map/ppermute | solution.py:25
  89.9 6.4 %collective-permute-done.2 = bf16[512,384]{1,0:T(8,128)(2,1)} collective-permute-done((bf16[512,384]{1,0:T(8,128)(2,1)}, bf16[512,384]{1,0:T(8,128)(2,1)}, u32[]{:S(2)}, u32[]{:S(2)}) %collective-permute-start.2) | collective-permute-done | bytes 393248 | tf_op jit(solution)/shard_map/ppermute | solution.py:22
  101.2 56.4 %while.18 = (s32[]{:T(128)}, f32[6,512]{1,0:T(8,128)S(1)}, f32[6,512]{1,0:T(8,128)S(1)}, f32[512,384]{0,1:T(8,128)S(1)}, bf16[2048,384]{0,1:T(8,128)(2,1)}, /*in...) while((s32[]{:T(128)}, f32[6,512]{1,0:T(8,128)S(1)}, ...), condition=%wide.region_7.8_spmd.clone, body=%wide.region_4.7_spmd.clone.sunk | while | flops 415844352 | bytes 25755828 | solution.py:81
  102.2 3.7 %bitcast_reduce_fusion.2 = (f32[6,512]{1,0:T(8,128)S(1)}, f32[6,512,512]{2,1,0:T(8,128)}) fusion(bf16[512,6,64]{0,2,1:T(8,128)(2,1)S(1)} %bitcast.78, bf16[512,6,64]{0,2,1:T(8,128)(2,1)S(1)} %get-tuple-element.312), kind=kOutput, calls=%fused_computation.1.clone.1 | convolution fusion | flops 204469248 | bytes 7090176 | tf_op jit(solution)/shard_map/while/body/eval_jaxpr/qhd,khd->hqk/dot_general | solution.py:54
  105.9 3.8 %fusion.90 = f32[6,512]{1,0:T(8,128)S(1)} fusion(f32[6,512,512]{2,1,0:T(8,128)} %get-tuple-element.283, f32[6,512]{1,0:T(8,128)S(1)} %get-tuple-element.308), kind=kLoop, calls=%fused_computation.4.clone.1 | loop fusion | flops 4715520 | bytes 6316032 | tf_op jit(solution)/shard_map/while/body/eval_jaxpr/reduce_sum | solution.py:60
  111.0 4.0 %fusion.92 = f32[6,64,512]{2,1,0:T(8,128)S(1)} fusion(bf16[512,6,64]{0,2,1:T(8,128)(2,1)S(1)} %bitcast.77, f32[6,512,512]{2,1,0:T(8,128)} %get-tuple-element.283, f32[6,512]{1,0:T(8,128)S(1)} %get-tuple-element.308), kind=kOutput, calls=%fused_computation.5.clone.1 | convolution fusion | flops 206045184 | bytes 7483392 | tf_op jit(solution)/shard_map/while/body/eval_jaxpr/hqk,khd->qhd/dot_general | solution.py:61
  120.0 3.8 %fusion.90 = f32[6,512]{1,0:T(8,128)S(1)} fusion(f32[6,512,512]{2,1,0:T(8,128)} %get-tuple-element.283, f32[6,512]{1,0:T(8,128)S(1)} %get-tuple-element.308), kind=kLoop, calls=%fused_computation.4.clone.1 | loop fusion | flops 4715520 | bytes 6316032 | tf_op jit(solution)/shard_map/while/body/eval_jaxpr/reduce_sum | solution.py:60
  125.1 4.0 %fusion.92 = f32[6,64,512]{2,1,0:T(8,128)S(1)} fusion(bf16[512,6,64]{0,2,1:T(8,128)(2,1)S(1)} %bitcast.77, f32[6,512,512]{2,1,0:T(8,128)} %get-tuple-element.283, f32[6,512]{1,0:T(8,128)S(1)} %get-tuple-element.308), kind=kOutput, calls=%fused_computation.5.clone.1 | convolution fusion | flops 206045184 | bytes 7483392 | tf_op jit(solution)/shard_map/while/body/eval_jaxpr/hqk,khd->qhd/dot_general | solution.py:61
  130.4 3.7 %bitcast_reduce_fusion.2 = (f32[6,512]{1,0:T(8,128)S(1)}, f32[6,512,512]{2,1,0:T(8,128)}) fusion(bf16[512,6,64]{0,2,1:T(8,128)(2,1)S(1)} %bitcast.78, bf16[512,6,64]{0,2,1:T(8,128)(2,1)S(1)} %get-tuple-element.312), kind=kOutput, calls=%fused_computation.1.clone.1 | convolution fusion | flops 204469248 | bytes 7090176 | tf_op jit(solution)/shard_map/while/body/eval_jaxpr/qhd,khd->hqk/dot_general | solution.py:54
  134.1 3.8 %fusion.90 = f32[6,512]{1,0:T(8,128)S(1)} fusion(f32[6,512,512]{2,1,0:T(8,128)} %get-tuple-element.283, f32[6,512]{1,0:T(8,128)S(1)} %get-tuple-element.308), kind=kLoop, calls=%fused_computation.4.clone.1 | loop fusion | flops 4715520 | bytes 6316032 | tf_op jit(solution)/shard_map/while/body/eval_jaxpr/reduce_sum | solution.py:60
  139.2 4.0 %fusion.92 = f32[6,64,512]{2,1,0:T(8,128)S(1)} fusion(bf16[512,6,64]{0,2,1:T(8,128)(2,1)S(1)} %bitcast.77, f32[6,512,512]{2,1,0:T(8,128)} %get-tuple-element.283, f32[6,512]{1,0:T(8,128)S(1)} %get-tuple-element.308), kind=kOutput, calls=%fused_computation.5.clone.1 | convolution fusion | flops 206045184 | bytes 7483392 | tf_op jit(solution)/shard_map/while/body/eval_jaxpr/hqk,khd->qhd/dot_general | solution.py:61
  144.5 3.7 %bitcast_reduce_fusion.2 = (f32[6,512]{1,0:T(8,128)S(1)}, f32[6,512,512]{2,1,0:T(8,128)}) fusion(bf16[512,6,64]{0,2,1:T(8,128)(2,1)S(1)} %bitcast.78, bf16[512,6,64]{0,2,1:T(8,128)(2,1)S(1)} %get-tuple-element.312), kind=kOutput, calls=%fused_computation.1.clone.1 | convolution fusion | flops 204469248 | bytes 7090176 | tf_op jit(solution)/shard_map/while/body/eval_jaxpr/qhd,khd->hqk/dot_general | solution.py:54
  148.2 3.8 %fusion.90 = f32[6,512]{1,0:T(8,128)S(1)} fusion(f32[6,512,512]{2,1,0:T(8,128)} %get-tuple-element.283, f32[6,512]{1,0:T(8,128)S(1)} %get-tuple-element.308), kind=kLoop, calls=%fused_computation.4.clone.1 | loop fusion | flops 4715520 | bytes 6316032 | tf_op jit(solution)/shard_map/while/body/eval_jaxpr/reduce_sum | solution.py:60
  153.3 4.0 %fusion.92 = f32[6,64,512]{2,1,0:T(8,128)S(1)} fusion(bf16[512,6,64]{0,2,1:T(8,128)(2,1)S(1)} %bitcast.77, f32[6,512,512]{2,1,0:T(8,128)} %get-tuple-element.283, f32[6,512]{1,0:T(8,128)S(1)} %get-tuple-element.308), kind=kOutput, calls=%fused_computation.5.clone.1 | convolution fusion | flops 206045184 | bytes 7483392 | tf_op jit(solution)/shard_map/while/body/eval_jaxpr/hqk,khd->qhd/dot_general | solution.py:61
  161.0 27.6 %reduce-scatter.7.cloned.1.call-done = bf16[384,512]{1,0:T(8,128)(2,1)} async-done(((bf16[1536,512]{1,0:T(8,128)(2,1)}), bf16[384,512]{1,0:T(8,128)(2,1)}) %reduce-scatter.7.cloned.1.call-update) | async-done | bytes 393232
  190.1 5.8 %all-reduce = (f32[512]{0:T(512)S(1)}, f32[512]{0:T(512)S(1)}) all-reduce(f32[512]{0:T(512)S(1)} %get-tuple-element.171, f32[512]{0:T(512)S(1)} %get-tuple-element.170), channel_id=1, replica_groups=mesh['parts'=2,'ctx'=4,'grid'=4] {'grid'}, use_global_device_ids=true, to_apply=%region_12.13 | all-reduce | flops 1024 | bytes 8192 | tf_op jit(solution)/shard_map/psum | solution.py:87
  197.0 20.7 %all-gather.8.cloned.1.call-done = bf16[512,1536]{1,0:T(8,128)(2,1)} async-done(((bf16[512,384]{1,0:T(8,128)(2,1)}), bf16[512,1536]{1,0:T(8,128)(2,1)}) %all-gather.8.cloned.1.call-update) | async-done | bytes 1572880 | tf_op jit(solution)/shard_map/all_gather | solution.py:94
  223.1 4.7 %collective-permute-start.3 = (bf16[15,384]{1,0:T(8,128)(2,1)S(1)}, bf16[15,384]{1,0:T(8,128)(2,1)S(1)}, u32[]{:S(2)}, u32[]{:S(2)}) collective-permute-start(bf16[15,384]{1,0:T(8,128)(2,1)S(1)} %get-tuple-element.228), channel_id=1, source_target_pairs={{0,4},{4,8},{8,12},{1,5},{5,9},{9,13},{2,6},{6,10},{10,14},{3,7},{... | collective-permute-start | bytes 34568 | tf_op jit(solution)/shard_map/ppermute | solution.py:40
  229.0 7.4 %fusion.11 = bf16[1536,512]{0,1:T(8,128)(2,1)S(1)} fusion(bf16[384,1536]{1,0:T(8,128)(2,1)S(1)} %copy-done.8, bf16[512,384]{1,0:T(8,128)(2,1)S(1)} %fusion.15, bf16[15,384]{1,0:T(8,128)(2,1)S(1)} %collective-permute-done.4, bf16[15,384]{1,0:T(8,128)(2,1)S(1)} %collective-permute-done.3, f32[384]{0:T(512)S(1)} %copy-done.9, f32[384]{0:T(512)S(1)} %copy-done.10, ...), kind=kOutput, calls=%fused_computation.21 | convolution fusion | flops 641925120 | bytes 3219456 | tf_op jit(solution)/shard_map/dot_general | solution.py:102
  238.0 29.2 %reduce-scatter.9.cloned.1.call-done = bf16[384,512]{1,0:T(8,128)(2,1)} async-done(((bf16[1536,512]{1,0:T(8,128)(2,1)}), bf16[384,512]{1,0:T(8,128)(2,1)}) %reduce-scatter.9.cloned.1.call-update) | async-done | bytes 393232
  (104 shorter events, 58.4 us)
Async XLA Ops:
  6.5 151.1 %copy-start = (bf16[384,1536]{1,0:T(8,128)(2,1)S(1)}, bf16[384,1536]{1,0:T(8,128)(2,1)}, u32[]{:S(2)}) copy-start(bf16[384,1536]{1,0:T(8,128)(2,1)} %param.23) | copy-start | bytes 3538948
  6.5 33.1 %all-gather.4.cloned.1.call-start = ((), (), s32[]{:S(2)}) async-start(), calls=%async_computation.2 | async-start | bytes 1966080 | tf_op jit(solution)/shard_map/all_gather | solution.py:94
  19.6 81.6 %all-gather.6.cloned.1.call-start = ((), (), s32[]{:S(2)}) async-start(), calls=%async_computation.3 | async-start | bytes 1966080 | tf_op jit(solution)/shard_map/all_gather | solution.py:148
  39.7 3.7 %copy-start.5 = (bf16[512,1536]{1,0:T(8,128)(2,1)S(1)}, bf16[512,1536]{1,0:T(8,128)(2,1)}, u32[]{:S(2)}) copy-start(bf16[512,1536]{1,0:T(8,128)(2,1)} %all-gather.4.cloned.1.call-done) | copy-start | bytes 4718596
  43.3 145.3 %reduce-scatter.7.cloned.1.call-start = ((), (), s32[]{:S(2)}) async-start(), calls=%async_computation.5 | async-start | bytes 1966080
  45.6 17.7 %collective-permute-start = (bf16[512,384]{1,0:T(8,128)(2,1)S(1)}, bf16[512,384]{1,0:T(8,128)(2,1)}, u32[]{:S(2)}, u32[]{:S(2)}) collective-permute-start(bf16[512,384]{1,0:T(8,128)(2,1)S(1)} %convolution_convert_fusion.4), channel_id=1, source_target_pairs={{0,4},{4,8},{8,12},{12,0},{1,5},{5,9},{9,13},{13,1},{2,6},{6,10},{... | collective-permute-start | bytes 1179656 | tf_op jit(solution)/shard_map/ppermute | solution.py:22
  47.2 39.9 %collective-permute-start.1 = (bf16[512,384]{1,0:T(8,128)(2,1)S(1)}, bf16[512,384]{1,0:T(8,128)(2,1)}, u32[]{:S(2)}, u32[]{:S(2)}) collective-permute-start(bf16[512,384]{1,0:T(8,128)(2,1)S(1)} %convolution_convert_fusion.4), channel_id=1, source_target_pairs={{0,12},{4,0},{8,4},{12,8},{1,13},{5,1},{9,5},{13,9},{2,14},{6,2},{... | collective-permute-start | bytes 1179656 | tf_op jit(solution)/shard_map/ppermute | solution.py:25
  63.3 33.1 %collective-permute-start.2 = (bf16[512,384]{1,0:T(8,128)(2,1)}, bf16[512,384]{1,0:T(8,128)(2,1)}, u32[]{:S(2)}, u32[]{:S(2)}) collective-permute-start(bf16[512,384]{1,0:T(8,128)(2,1)} %collective-permute-done), channel_id=1, source_target_pairs={{0,4},{4,8},{8,12},{12,0},{1,5},{5,9},{9,13},{13,1},{2,6},{6,10},{... | collective-permute-start | bytes 1179656 | tf_op jit(solution)/shard_map/ppermute | solution.py:22
  160.3 0.7 copy-start.3
  160.3 0.7 copy-start.4
  160.3 29.5 %copy-start.1 = (bf16[512,384]{1,0:T(8,128)(2,1)S(1)}, bf16[512,384]{1,0:T(8,128)(2,1)}, u32[]{:S(2)}) copy-start(bf16[512,384]{1,0:T(8,128)(2,1)} %param.17) | copy-start | bytes 1179652
  160.3 57.4 %all-gather.8.cloned.1.call-start = ((), (), s32[]{:S(2)}) async-start(), calls=%async_computation.4 | async-start | bytes 1966080 | tf_op jit(solution)/shard_map/all_gather | solution.py:94
  161.0 35.9 %copy-start.2 = (f32[31,384]{1,0:T(8,128)S(1)}, f32[31,384]{1,0:T(8,128)}, u32[]{:S(2)}) copy-start(f32[31,384]{1,0:T(8,128)} %param.28) | copy-start | bytes 142852
  196.9 70.4 %reduce-scatter.9.cloned.1.call-start = ((), (), s32[]{:S(2)}) async-start(), calls=%async_computation.6 | async-start | bytes 1966080
  217.8 3.0 %copy-start.6 = (bf16[512,1536]{1,0:T(8,128)(2,1)S(1)}, bf16[512,1536]{1,0:T(8,128)(2,1)}, u32[]{:S(2)}) copy-start(bf16[512,1536]{1,0:T(8,128)(2,1)} %all-gather.8.cloned.1.call-done) | copy-start | bytes 4718596
  217.8 3.0 %copy-start.7 = (bf16[1536,384]{1,0:T(8,128)(2,1)S(1)}, bf16[1536,384]{1,0:T(8,128)(2,1)}, u32[]{:S(2)}) copy-start(bf16[1536,384]{1,0:T(8,128)(2,1)} %param.26) | copy-start | bytes 3538948
  220.8 8.3 %copy-start.8 = (bf16[384,1536]{1,0:T(8,128)(2,1)S(1)}, bf16[384,1536]{1,0:T(8,128)(2,1)}, u32[]{:S(2)}) copy-start(bf16[384,1536]{1,0:T(8,128)(2,1)} %param.31) | copy-start | bytes 3538948
  220.8 8.3 %copy-start.9 = (f32[384]{0:T(512)S(1)}, f32[384]{0:T(512)}, u32[]{:S(2)}) copy-start(f32[384]{0:T(512)} %param.30) | copy-start | bytes 4612
  220.8 8.3 %copy-start.10 = (f32[384]{0:T(512)S(1)}, f32[384]{0:T(512)}, u32[]{:S(2)}) copy-start(f32[384]{0:T(512)} %param.29) | copy-start | bytes 4612
  221.8 6.1 %collective-permute-start.4 = (bf16[15,384]{1,0:T(8,128)(2,1)S(1)}, bf16[15,384]{1,0:T(8,128)(2,1)S(1)}, u32[]{:S(2)}, u32[]{:S(2)}) collective-permute-start(bf16[15,384]{1,0:T(8,128)(2,1)S(1)} %get-tuple-element.229), channel_id=1, source_target_pairs={{4,0},{8,4},{12,8},{5,1},{9,5},{13,9},{6,2},{10,6},{14,10},{7,3},{... | collective-permute-start | bytes 34568 | tf_op jit(solution)/shard_map/ppermute | solution.py:42
  223.1 5.9 %collective-permute-start.3 = (bf16[15,384]{1,0:T(8,128)(2,1)S(1)}, bf16[15,384]{1,0:T(8,128)(2,1)S(1)}, u32[]{:S(2)}, u32[]{:S(2)}) collective-permute-start(bf16[15,384]{1,0:T(8,128)(2,1)S(1)} %get-tuple-element.228), channel_id=1, source_target_pairs={{0,4},{4,8},{8,12},{1,5},{5,9},{9,13},{2,6},{6,10},{10,14},{3,7},{... | collective-permute-start | bytes 34568 | tf_op jit(solution)/shard_map/ppermute | solution.py:40
Sparse Core Ops, SparseCore 0:
  19.7 19.9 all-gather.3
  43.4 57.7 all-gather.5
  160.5 28.1 reduce-scatter.6
  197.0 20.7 all-gather.7
  238.2 29.0 reduce-scatter.8
